TPU v7x, 512 devices: a whole 4x4x16 slice. The times are simulated.
512 devices in a mesh: gx: 64 (over z_lo, x, core), yz: 8 (over y, z_hi).
Axes of the slice: x: 4, y: 4, z: 16 (z_hi: 2, z_lo: 8; z = z_hi * 8 + z_lo), core: 2. Of those that a mesh axis runs over, the one named last changes fastest.
Arguments:
- solution: float32 [4, 512, 64, 3, 128], P(None, 'gx', 'yz'), may hold values from -6 to 6
- residual: float32 [4, 512, 64, 3, 128], P(None, 'gx', 'yz'), may hold values from -6 to 6
- direction: float32 [4, 512, 64, 3, 128], P(None, 'gx', 'yz'), may hold values from -6 to 6
- stiffness: float32 [512, 64, 128], P('gx', 'yz'), may hold values from 0.5 to 13.52
- coupling: float32 [512, 64, 128], P('gx', 'yz'), may hold values from 0.5 to 2
- lower_factor: float32 [64, 8, 384, 384], P('gx', 'yz'), may hold values from -0.122474487 to 1
- upper_factor: float32 [64, 8, 384, 384], P('gx', 'yz'), may hold values from -0.122474487 to 2, as said below
- pivot_order: int32 [64, 8, 384], P('gx', 'yz'), may hold values from 0 to 383, each once within a row
- coarse_basis: float32 [4, 512, 64, 128], P(None, 'gx', 'yz'), may hold values from 0.2 to 1
- coarse_inverse: float32 [64, 8, 12, 6144], P('gx', 'yz'), may hold values from -0.00024917498 to 0.009765625
- inner_prior: float32 [4], replicated, may hold values from 6291456 to 25165824
Outputs:
- solution_next: float32 [4, 512, 64, 3, 128], P(None, 'gx', 'yz')
- residual_next: float32 [4, 512, 64, 3, 128], P(None, 'gx', 'yz')
- direction_next: float32 [4, 512, 64, 3, 128], P(None, 'gx', 'yz')
- inner_next: float32 [4], replicated
Inputs may be any that keep to these rules, and one draw needn't show every extreme that they name: `upper_factor`: upper triangular with positive diagonal.
All inputs are finite; a program needn't handle non-finite values.
Results may differ from a plain program's by a relative error of at most 0.000067.
Values sent between devices are 32-bit elements; how exact they have to be, the bound alone decides.
No kernel may reach another device: no remote copies, remote signals or barrier semaphores. Data moves between devices by JAX's collectives and lax.ppermute only.
A program may use at most 64 MiB of HBM per device.

v0:
```python
import jax
import jax.numpy as jnp
from jax import lax
from jax.sharding import PartitionSpec as P

precise = lax.Precision.HIGHEST


def with_halo(cells, sides, width):
    for axis, dim in sides:
        count = lax.axis_size(axis)
        ends = count - 1
        head = lax.slice_in_dim(cells, 0, width, axis=dim)
        tail = lax.slice_in_dim(cells, cells.shape[dim] - width, cells.shape[dim], axis=dim)
        cells = jnp.concatenate(
            [
                lax.ppermute(tail, axis, [(i, (i + 1) % count) for i in range(ends)]),
                cells,
                lax.ppermute(head, axis, [((i + 1) % count, i) for i in range(ends)]),
            ],
            axis=dim,
        )
    return cells


def stencil(padded, scaled):
    zero_plane = jnp.zeros_like(scaled[..., :1])
    upward = jnp.concatenate([scaled[..., 1:], zero_plane], axis=4)
    downward = jnp.concatenate([zero_plane, scaled[..., :-1]], axis=4)
    beside = padded[:, 2:, 1:-1] + padded[:, :-2, 1:-1] + padded[:, 1:-1, 2:] + padded[:, 1:-1, :-2]
    return 6.0 * scaled - beside - upward - downward


def operate(direction, stiffness, coupling):
    scaled = stiffness[None, :, :, None, :] * direction
    padded = with_halo(scaled, (("gx", 1), ("yz", 2)), 1)
    return stiffness[None, :, :, None, :] * stencil(padded, scaled) + coupling[
        None, :, :, None, :
    ] * jnp.sum(direction, axis=3, keepdims=True)


def local_solve(field, lower_factor, upper_factor, pivot_order):
    line_width = lower_factor.shape[-1]
    line_rows = field.reshape(-1, line_width)
    pivots = pivot_order.reshape(line_width)
    inverse_order = jnp.argsort(pivots)
    permuted = jnp.take(line_rows, pivots, axis=1)
    middle = jnp.dot(
        permuted, lower_factor[0, 0].T, precision=precise, preferred_element_type=jnp.float32
    )
    solved = jnp.dot(
        middle, upper_factor[0, 0].T, precision=precise, preferred_element_type=jnp.float32
    )
    return jnp.take(solved, inverse_order, axis=1).reshape(field.shape)


def across(padded, field):
    field_shape = field.shape
    blank_rows = jnp.zeros(field_shape[:1] + (field_shape[1] - 2,) + field_shape[2:], field.dtype)
    across_first = jnp.concatenate([padded[:, :1, 1:-1], blank_rows, padded[:, -1:, 1:-1]], axis=1)
    blank_cols = jnp.zeros(field_shape[:2] + (field_shape[2] - 2,) + field_shape[3:], field.dtype)
    across_second = jnp.concatenate([padded[:, 1:-1, :1], blank_cols, padded[:, 1:-1, -1:]], axis=2)
    return field + 0.5 * (across_first + across_second)


def restrict(coarse_basis, field):
    weighted = jnp.einsum("pxyz,cxykz->ckp", coarse_basis, field, precision=precise)
    return weighted.reshape(field.shape[0], -1)


def prolong(coarse_basis, coarse_values, field_shape):
    shaped = coarse_values.reshape(field_shape[0], field_shape[3], coarse_basis.shape[0])
    return jnp.einsum("pxyz,ckp->cxykz", coarse_basis, shaped, precision=precise)


def per_device(
    solution,
    residual,
    direction,
    stiffness,
    coupling,
    lower_factor,
    upper_factor,
    pivot_order,
    coarse_basis,
    coarse_inverse,
    inner_prior,
):
    case_count = residual.shape[0]
    applied = operate(direction, stiffness, coupling)
    curve_part = jnp.sum(direction * applied, axis=(1, 2, 3, 4))
    curvature = lax.psum(curve_part, ("gx", "yz"))
    step_size = inner_prior / curvature
    step_field = step_size[:, None, None, None, None]
    residual_next = residual - step_field * applied
    primal = restrict(coarse_basis, residual_next)
    primal_all = lax.all_gather(primal[:, None, :], ("gx", "yz"), axis=1, tiled=True).reshape(
        case_count, -1
    )
    coarse_values = jnp.dot(
        primal_all, coarse_inverse[0, 0].T, precision=precise, preferred_element_type=jnp.float32
    )
    correction = prolong(coarse_basis, coarse_values, residual.shape)
    local_part = local_solve(residual_next, lower_factor, upper_factor, pivot_order)
    padded = with_halo(local_part, (("gx", 1), ("yz", 2)), 1)
    smoothed = across(padded, local_part)
    preconditioned = smoothed + correction
    inner_part = jnp.sum(residual_next * preconditioned, axis=(1, 2, 3, 4))
    inner_next = lax.psum(inner_part, ("gx", "yz"))
    growth = (inner_next / inner_prior)[:, None, None, None, None]
    direction_next = preconditioned + growth * direction
    solution_next = solution + step_field * direction
    return (solution_next, residual_next, direction_next, inner_next)


def solution(mesh):
    in_specs = (
        P(None, "gx", "yz", None, None),
        P(None, "gx", "yz", None, None),
        P(None, "gx", "yz", None, None),
        P("gx", "yz", None),
        P("gx", "yz", None),
        P("gx", "yz", None, None),
        P("gx", "yz", None, None),
        P("gx", "yz", None),
        P(None, "gx", "yz", None),
        P("gx", "yz", None, None),
        P(),
    )
    out_specs = (
        P(None, "gx", "yz", None, None),
        P(None, "gx", "yz", None, None),
        P(None, "gx", "yz", None, None),
        P(),
    )
    return jax.shard_map(
        per_device, mesh=mesh, in_specs=in_specs, out_specs=out_specs, check_vma=False
    )
```

profile of v0, /device:TPU:1, one launch (start us, length us, event | category | flops | bytes accessed | tf_op | source)
XLA Modules:
  0.0 2391.1 jit_solution(16158936149588700655)
XLA Ops:
  0.6 1.3 copy_multiply_fusion
  2.0 8.7 collective-permute-start
  10.8 2.1 collective-permute-start.1
  13.2 3.8 sort.17
  18.1 11.2 collective-permute-start.3
  29.3 1.3 collective-permute-start.2
  30.6 3.7 collective-permute-done.3
  34.3 10.0 collective-permute-done.2
  45.0 103.4 %psum.14 = f32[4]{0:T(128)S(1)} all-reduce(f32[4]{0:T(128)S(1)} %get-tuple-element.19), channel_id=1, replica_groups=mesh['gx'=64,'yz'=8] {'gx','yz'}, use_global_device_ids=true, to_apply=%region_2.0 | all-reduce | flops 4 | bytes 32 | tf_op jit(solution)/shard_map/psum | solution.py:92
  148.9 0.8 copy-done.8
  149.7 1.6 convolution_bitcast_fusion.1
  151.6 1.7 gather_fusion
  153.3 1.5 fusion.2
  154.8 0.8 fusion
  155.6 1.7 gather_fusion.1
  157.6 2.6 collective-permute-start.4
  160.2 2047.1 %all_gather.3 = f32[4,512,12]{2,0,1:T(4,128)S(1)} all-gather(f32[4,1,12]{2,0,1:T(4,128)S(1)} %broadcast_in_dim_reshape.3), channel_id=1, replica_groups=mesh['gx'=64,'yz'=8] {'gx','yz'}, dimensions={1}, use_global_device_ids=true | all-gather | bytes 98496 | tf_op jit(solution)/shard_map/all_gather | solution.py:97
  2208.1 1.9 collective-permute-start.5
  2210.4 15.4 collective-permute-done.5
  2225.8 1.3 collective-permute-start.7
  2227.1 12.9 collective-permute-start.6
  2240.0 3.3 convolution_bitcast_fusion.2
  2243.3 1.0 multiply_reduce_fusion
  2244.3 144.2 %psum.15 = f32[4]{0:T(128)S(1)} all-reduce(f32[4]{0:T(128)S(1)} %get-tuple-element.33), channel_id=1, replica_groups=mesh['gx'=64,'yz'=8] {'gx','yz'}, use_global_device_ids=true, to_apply=%region_5.7 | all-reduce | flops 4 | bytes 32 | tf_op jit(solution)/shard_map/psum | solution.py:109
  (71 shorter events, 6.9 us)
Async XLA Ops:
  0.6 152.6 %copy-start = (f32[1,1,384,384]{3,2,1,0:T(8,128)S(1)}, f32[1,1,384,384]{3,2,1,0:T(8,128)}, u32[]{:S(2)}) copy-start(f32[1,1,384,384]{3,2,1,0:T(8,128)} %param.18) | copy-start | bytes 1769476
  2.0 16.1 collective-permute-start
  10.8 2.4 copy-start.10
  10.8 2.4 copy-start.1
  10.8 7.3 collective-permute-start.1
  13.2 3.8 copy-start.9
  13.2 3.9 copy-start.6
  18.1 26.2 %copy-start.7 = (f32[8,8,128]{2,1,0:T(8,128)S(1)}, f32[8,8,128]{2,1,0:T(8,128)}, u32[]{:S(2)}) copy-start(f32[8,8,128]{2,1,0:T(8,128)} %param.16) | copy-start | bytes 98308
  18.1 16.2 collective-permute-start.3
  29.3 15.0 collective-permute-start.2
  44.3 104.2 %copy-start.5 = (f32[4,8,8,3,128]{4,2,3,1,0:T(8,128)S(1)}, f32[4,8,8,3,128]{4,2,3,1,0:T(8,128)}, u32[]{:S(2)}) copy-start(f32[4,8,8,3,128]{4,2,3,1,0:T(8,128)} %param.14) | copy-start | bytes 1179652
  45.0 103.5 %copy-start.11 = (f32[4]{0:T(128)S(1)}, f32[4]{0:T(128)}, u32[]{:S(2)}) copy-start(f32[4]{0:T(128)} %param.23) | copy-start | bytes 52
  148.8 0.9 copy-start.8
  148.9 2.7 copy-start.2
  153.3 1.5 copy-start.3
  157.6 2052.4 %collective-permute-start.4 = (f32[4,1,8,3,128]{4,0,2,1,3:T(4,128)S(1)}, f32[4,1,8,3,128]{4,0,2,1,3:T(4,128)S(1)}, u32[]{:S(2)}, u32[]{:S(2)}) collective-permute-start(f32[4,1,8,3,128]{4,0,2,1,3:T(4,128)S(1)} %copy.96), channel_id=1, source_target_pairs={{0,8},{8,16},{16,24},{24,32},{32,40},{40,48},{48,56},{56,64},{64,7... | collective-permute-start | bytes 147464 | tf_op jit(solution)/shard_map/ppermute | solution.py:17
  2208.1 17.6 collective-permute-start.5
  2225.8 17.5 collective-permute-start.7
  2227.1 16.2 collective-permute-start.6
  2243.3 145.7 %copy-start.4 = (f32[4,8,8,3,128]{4,2,3,1,0:T(8,128)S(1)}, f32[4,8,8,3,128]{4,2,3,1,0:T(8,128)}, u32[]{:S(2)}) copy-start(f32[4,8,8,3,128]{4,2,3,1,0:T(8,128)} %param.13) | copy-start | bytes 1179652
  2388.5 0.5 copy-start.12
where the time goes:
time: 2390 us
  blocking collectives  2290 us (96%)
  starting transfers between devices  42 us (2%)
  waiting for transfers between devices  29.1 us (1%)
    all_gather x1, blocking collectives, per_device(): lax.all_gather(primal[:, None, :], ('gx', 'yz'), axis=1, tiled=True)  2050 us
    psum x1, blocking collectives, per_device(): inner_next = lax.psum(inner_part, ('gx', 'yz'))  144 us
    psum x1, blocking collectives, per_device(): curvature = lax.psum(curve_part, ('gx', 'yz'))  103 us
  transfers between devices with their start and end apart: 8, of which 3 were waited for; matrix products, arithmetic and copies ran while one was open for 0% of the time, Pallas kernels for 0%

commit v1 on v0

--- a/solution.py
+++ b/solution.py
@@ -94,9 +94,12 @@
     step_field = step_size[:, None, None, None, None]
     residual_next = residual - step_field * applied
     primal = restrict(coarse_basis, residual_next)
-    primal_all = lax.all_gather(primal[:, None, :], ("gx", "yz"), axis=1, tiled=True).reshape(
-        case_count, -1
-    )
+    primal_all = jnp.concatenate(
+        lax.all_to_all(
+            jnp.stack([primal[:, None, :]] * lax.axis_size(("gx", "yz"))), ("gx", "yz"), 0, 0
+        ),
+        axis=1,
+    ).reshape(case_count, -1)
     coarse_values = jnp.dot(
         primal_all, coarse_inverse[0, 0].T, precision=precise, preferred_element_type=jnp.float32
     )

time: 2390 us -> 363 us (0.15)
  blocking collectives: 2290 us -> 225 us
    all_gather x1 -> x0, blocking collectives: 2050 us -> none  [per_device(): lax.all_gather(primal[:, None, :], ('gx', 'yz'), axis=1, tiled=True)]
  transfers between devices with their start and end apart: 8 -> 9, of which waited for: 3 -> 4; matrix products, arithmetic and copies ran while one was open for 0% -> 2% of each run, Pallas kernels for 0% -> 0%
where the time goes in v1:
time: 363 us; the launch traced here: 362 us
  blocking collectives  225 us (62%)
  starting transfers between devices  60.2 us (17%)
  waiting for transfers between devices  48 us (13%)
  local copies, waits for them, and re-layouts  11.6 us (3%)
  matrix products  8.19 us (2%)
  other arithmetic  7.68 us (2%)
    psum x1, blocking collectives, per_device(): inner_next = lax.psum(inner_part, ('gx', 'yz'))  122 us
    psum x1, blocking collectives, per_device(): curvature = lax.psum(curve_part, ('gx', 'yz'))  104 us
    ppermute x4, waiting for transfers between devices, with_halo(): lax.ppermute(head, axis, [((i + 1) % count, i) for i in range(ends)])  44.3 us
    ppermute x4, starting transfers between devices, with_halo(): lax.ppermute(tail, axis, [(i, (i + 1) % count) for i in range(ends)])  29 us
    ppermute x4, starting transfers between devices, with_halo(): lax.ppermute(head, axis, [((i + 1) % count, i) for i in range(ends)])  17.5 us
    all_to_all x1, starting transfers between devices, per_device(): lax.all_to_all(jnp.stack([primal[:, None, :]] * lax.axis_size(('gx', 'yz'...  13.7 us
  transfers between devices with their start and end apart: 9, of which 4 were waited for; matrix products, arithmetic and copies ran while one was open for 2% of the time, Pallas kernels for 0%

profile of v1, /device:TPU:1, one launch (start us, length us, event | category | flops | bytes accessed | tf_op | source)
XLA Modules:
  0.0 362.1 jit_solution(15280283728341117921)
XLA Ops:
  0.6 1.3 copy_multiply_fusion
  2.0 8.7 %collective-permute-start = (f32[4,1,8,3,128]{4,0,2,1,3:T(4,128)S(1)}, f32[4,1,8,3,128]{4,0,2,1,3:T(4,128)S(1)}, u32[]{:S(2)}, u32[]{:S(2)}) collective-permute-start(f32[4,1,8,3,128]{4,0,2,1,3:T(4,128)S(1)} %get-tuple-element.30), channel_id=1, source_target_pairs={{8,0},{16,8},{24,16},{32,24},{40,32},{48,40},{56,48},{64,56},{72,6... | collective-permute-start | bytes 147464 | tf_op jit(solution)/shard_map/ppermute | solution.py:19
  10.8 2.1 collective-permute-start.1
  13.2 3.8 %sort.17 = (s32[384]{0:T(512)}, s32[384]{0:T(512)S(1)}) sort(s32[384]{0:T(512)S(1)} %reduce, s32[384]{0:T(512)S(1)} %iota.4), dimensions={0}, to_apply=%region_3.5 | sort | flops 3456 | bytes 6144 | tf_op jit(solution)/shard_map/jit(argsort)/sort | solution.py:46
  17.2 11.2 %collective-permute-start.3 = (f32[4,10,1,3,128]{4,0,2,1,3:T(4,128)S(1)}, f32[4,10,1,3,128]{4,0,2,1,3:T(4,128)S(1)}, u32[]{:S(2)}, u32[]{:S(2)}) collective-permute-start(f32[4,10,1,3,128]{4,0,2,1,3:T(4,128)S(1)} %get-tuple-element.24), channel_id=1, source_target_pairs={{0,1},{1,2},{2,3},{3,4},{4,5},{5,6},{6,7},{8,9},{9,10},{10,11},{11... | collective-permute-start | bytes 184328 | tf_op jit(solution)/shard_map/ppermute | solution.py:17
  28.4 1.3 collective-permute-start.2
  29.7 3.7 %collective-permute-done.3 = f32[4,10,1,3,128]{4,0,2,1,3:T(4,128)S(1)} collective-permute-done((f32[4,10,1,3,128]{4,0,2,1,3:T(4,128)S(1)}, f32[4,10,1,3,128]{4,0,2,1,3:T(4,128)S(1)}, u32[]{:S(2)}, u32[]{:S(2)}) %collective-permute-start.3) | collective-permute-done | bytes 61472 | tf_op jit(solution)/shard_map/ppermute | solution.py:17
  33.4 10.4 %collective-permute-done.2 = f32[4,10,1,3,128]{4,0,2,1,3:T(4,128)S(1)} collective-permute-done((f32[4,10,1,3,128]{4,0,2,1,3:T(4,128)S(1)}, f32[4,10,1,3,128]{4,0,2,1,3:T(4,128)S(1)}, u32[]{:S(2)}, u32[]{:S(2)}) %collective-permute-start.2) | collective-permute-done | bytes 61472 | tf_op jit(solution)/shard_map/ppermute | solution.py:19
  44.6 103.7 %psum.14 = f32[4]{0:T(128)S(1)} all-reduce(f32[4]{0:T(128)S(1)} %get-tuple-element.19), channel_id=1, replica_groups=mesh['gx'=64,'yz'=8] {'gx','yz'}, use_global_device_ids=true, to_apply=%region_2.0 | all-reduce | flops 4 | bytes 32 | tf_op jit(solution)/shard_map/psum | solution.py:92
  149.6 1.7 gather_fusion
  151.2 1.5 fusion.2
  153.6 1.7 gather_fusion.1
  155.6 2.1 collective-permute-start.4
  157.7 1.6 convolution_bitcast_fusion.1
  159.4 1.1 stack.3
  160.5 13.7 %all-to-all-start = ((f32[512,4,1,12]{3,1,2,0:T(4,128)}), f32[512,4,1,12]{3,1,2,0:T(4,128)S(1)}, u32[]{:S(2)}, u32[]{:S(2)}) async-start(f32[512,4,1,12]{3,1,2,0:T(4,128)} %stack.3), calls=%async_computation | async-start | bytes 2097152 | tf_op jit(solution)/shard_map/all_to_all | solution.py:98
  174.2 6.2 %collective-permute-start.5 = (f32[4,1,8,3,128]{4,0,2,1,3:T(4,128)S(1)}, f32[4,1,8,3,128]{4,0,2,1,3:T(4,128)S(1)}, u32[]{:S(2)}, u32[]{:S(2)}) collective-permute-start(f32[4,1,8,3,128]{4,0,2,1,3:T(4,128)S(1)} %copy.94), channel_id=1, source_target_pairs={{8,0},{16,8},{24,16},{32,24},{40,32},{48,40},{56,48},{64,56},{72,6... | collective-permute-start | bytes 147464 | tf_op jit(solution)/shard_map/ppermute | solution.py:19
  181.3 1.3 collective-permute-start.7
  182.6 13.7 %collective-permute-start.6 = (f32[4,10,1,3,128]{4,0,2,1,3:T(4,128)S(1)}, f32[4,10,1,3,128]{4,0,2,1,3:T(4,128)S(1)}, u32[]{:S(2)}, u32[]{:S(2)}) collective-permute-start(f32[4,10,1,3,128]{4,0,2,1,3:T(4,128)S(1)} %get-tuple-element.21), channel_id=1, source_target_pairs={{0,1},{1,2},{2,3},{3,4},{4,5},{5,6},{6,7},{8,9},{9,10},{10,11},{11... | collective-permute-start | bytes 184328 | tf_op jit(solution)/shard_map/ppermute | solution.py:17
  197.0 0.8 dot_general.20
  197.9 33.4 %collective-permute-done.7 = f32[4,10,1,3,128]{4,0,2,1,3:T(4,128)S(1)} collective-permute-done((f32[4,10,1,3,128]{4,0,2,1,3:T(4,128)S(1)}, f32[4,10,1,3,128]{4,0,2,1,3:T(4,128)S(1)}, u32[]{:S(2)}, u32[]{:S(2)}) %collective-permute-start.7) | collective-permute-done | bytes 61472 | tf_op jit(solution)/shard_map/ppermute | solution.py:19
  233.6 3.3 convolution_bitcast_fusion.2
  236.9 1.0 multiply_reduce_fusion
  238.0 121.5 %psum.15 = f32[4]{0:T(128)S(1)} all-reduce(f32[4]{0:T(128)S(1)} %get-tuple-element.33), channel_id=1, replica_groups=mesh['gx'=64,'yz'=8] {'gx','yz'}, use_global_device_ids=true, to_apply=%region_5.7 | all-reduce | flops 4 | bytes 32 | tf_op jit(solution)/shard_map/psum | solution.py:112
  (89 shorter events, 10.2 us)
Async XLA Ops:
  0.6 150.6 %copy-start = (f32[1,1,384,384]{3,2,1,0:T(8,128)S(1)}, f32[1,1,384,384]{3,2,1,0:T(8,128)}, u32[]{:S(2)}) copy-start(f32[1,1,384,384]{3,2,1,0:T(8,128)} %param.18) | copy-start | bytes 1769476
  2.0 15.1 %collective-permute-start = (f32[4,1,8,3,128]{4,0,2,1,3:T(4,128)S(1)}, f32[4,1,8,3,128]{4,0,2,1,3:T(4,128)S(1)}, u32[]{:S(2)}, u32[]{:S(2)}) collective-permute-start(f32[4,1,8,3,128]{4,0,2,1,3:T(4,128)S(1)} %get-tuple-element.30), channel_id=1, source_target_pairs={{8,0},{16,8},{24,16},{32,24},{40,32},{48,40},{56,48},{64,56},{72,6... | collective-permute-start | bytes 147464 | tf_op jit(solution)/shard_map/ppermute | solution.py:19
  10.8 2.4 copy-start.17
  10.8 2.4 copy-start.1
  10.8 6.4 %collective-permute-start.1 = (f32[4,1,8,3,128]{4,0,2,1,3:T(4,128)S(1)}, f32[4,1,8,3,128]{4,0,2,1,3:T(4,128)S(1)}, u32[]{:S(2)}, u32[]{:S(2)}) collective-permute-start(f32[4,1,8,3,128]{4,0,2,1,3:T(4,128)S(1)} %get-tuple-element.29), channel_id=1, source_target_pairs={{0,8},{8,16},{16,24},{24,32},{32,40},{40,48},{48,56},{56,64},{64,7... | collective-permute-start | bytes 147464 | tf_op jit(solution)/shard_map/ppermute | solution.py:17
  13.2 3.8 %copy-start.16 = (f32[8,8,128]{2,1,0:T(8,128)S(1)}, f32[8,8,128]{2,1,0:T(8,128)}, u32[]{:S(2)}) copy-start(f32[8,8,128]{2,1,0:T(8,128)} %param.17) | copy-start | bytes 98308
  17.2 26.7 %copy-start.12 = (f32[8,8,128]{2,1,0:T(8,128)S(1)}, f32[8,8,128]{2,1,0:T(8,128)}, u32[]{:S(2)}) copy-start(f32[8,8,128]{2,1,0:T(8,128)} %param.16) | copy-start | bytes 98308
  17.2 16.2 %collective-permute-start.3 = (f32[4,10,1,3,128]{4,0,2,1,3:T(4,128)S(1)}, f32[4,10,1,3,128]{4,0,2,1,3:T(4,128)S(1)}, u32[]{:S(2)}, u32[]{:S(2)}) collective-permute-start(f32[4,10,1,3,128]{4,0,2,1,3:T(4,128)S(1)} %get-tuple-element.24), channel_id=1, source_target_pairs={{0,1},{1,2},{2,3},{3,4},{4,5},{5,6},{6,7},{8,9},{9,10},{10,11},{11... | collective-permute-start | bytes 184328 | tf_op jit(solution)/shard_map/ppermute | solution.py:17
  28.4 15.5 %collective-permute-start.2 = (f32[4,10,1,3,128]{4,0,2,1,3:T(4,128)S(1)}, f32[4,10,1,3,128]{4,0,2,1,3:T(4,128)S(1)}, u32[]{:S(2)}, u32[]{:S(2)}) collective-permute-start(f32[4,10,1,3,128]{4,0,2,1,3:T(4,128)S(1)} %get-tuple-element.23), channel_id=1, source_target_pairs={{1,0},{2,1},{3,2},{4,3},{5,4},{6,5},{7,6},{9,8},{10,9},{11,10},{12... | collective-permute-start | bytes 184328 | tf_op jit(solution)/shard_map/ppermute | solution.py:19
  43.9 104.5 %copy-start.10 = (f32[4,8,8,3,128]{4,2,3,1,0:T(8,128)S(1)}, f32[4,8,8,3,128]{4,2,3,1,0:T(8,128)}, u32[]{:S(2)}) copy-start(f32[4,8,8,3,128]{4,2,3,1,0:T(8,128)} %param.14) | copy-start | bytes 1179652
  44.6 103.8 %copy-start.18 = (f32[4]{0:T(128)S(1)}, f32[4]{0:T(128)}, u32[]{:S(2)}) copy-start(f32[4]{0:T(128)} %param.23) | copy-start | bytes 52
  148.7 9.0 %copy-start.2 = (f32[4,8,8,3,128]{4,0,2,1,3:T(4,128)}, f32[4,8,8,3,128]{4,0,2,1,3:T(4,128)S(1)}, u32[]{:S(2)}) copy-start(f32[4,8,8,3,128]{4,0,2,1,3:T(4,128)S(1)} %copy_subtract_fusion) | copy-start | bytes 1179652
  155.5 24.9 %copy-start.4 = (f32[256,384]{1,0:T(8,128)}, f32[256,384]{1,0:T(8,128)S(1)}, u32[]{:S(2)}) copy-start(f32[256,384]{1,0:T(8,128)S(1)} %copy.57) | copy-start | bytes 1179652
  155.6 24.8 %collective-permute-start.4 = (f32[4,1,8,3,128]{4,0,2,1,3:T(4,128)S(1)}, f32[4,1,8,3,128]{4,0,2,1,3:T(4,128)S(1)}, u32[]{:S(2)}, u32[]{:S(2)}) collective-permute-start(f32[4,1,8,3,128]{4,0,2,1,3:T(4,128)S(1)} %copy.95), channel_id=1, source_target_pairs={{0,8},{8,16},{16,24},{24,32},{32,40},{40,48},{48,56},{56,64},{64,7... | collective-permute-start | bytes 147464 | tf_op jit(solution)/shard_map/ppermute | solution.py:17
  160.5 72.1 %all-to-all-start = ((f32[512,4,1,12]{3,1,2,0:T(4,128)}), f32[512,4,1,12]{3,1,2,0:T(4,128)S(1)}, u32[]{:S(2)}, u32[]{:S(2)}) async-start(f32[512,4,1,12]{3,1,2,0:T(4,128)} %stack.3), calls=%async_computation | async-start | bytes 2097152 | tf_op jit(solution)/shard_map/all_to_all | solution.py:98
  174.2 7.1 %collective-permute-start.5 = (f32[4,1,8,3,128]{4,0,2,1,3:T(4,128)S(1)}, f32[4,1,8,3,128]{4,0,2,1,3:T(4,128)S(1)}, u32[]{:S(2)}, u32[]{:S(2)}) collective-permute-start(f32[4,1,8,3,128]{4,0,2,1,3:T(4,128)S(1)} %copy.94), channel_id=1, source_target_pairs={{8,0},{16,8},{24,16},{32,24},{40,32},{48,40},{56,48},{64,56},{72,6... | collective-permute-start | bytes 147464 | tf_op jit(solution)/shard_map/ppermute | solution.py:19
  180.8 15.6 %copy-start.11 = (f32[1,1,12,6144]{3,1,2,0:T(1,128)S(1)}, f32[1,1,12,6144]{3,1,2,0:T(1,128)}, u32[]{:S(2)}) copy-start(f32[1,1,12,6144]{3,1,2,0:T(1,128)} %param.22) | copy-start | bytes 884740
  181.3 50.0 %collective-permute-start.7 = (f32[4,10,1,3,128]{4,0,2,1,3:T(4,128)S(1)}, f32[4,10,1,3,128]{4,0,2,1,3:T(4,128)S(1)}, u32[]{:S(2)}, u32[]{:S(2)}) collective-permute-start(f32[4,10,1,3,128]{4,0,2,1,3:T(4,128)S(1)} %get-tuple-element.22), channel_id=1, source_target_pairs={{1,0},{2,1},{3,2},{4,3},{5,4},{6,5},{7,6},{9,8},{10,9},{11,10},{12... | collective-permute-start | bytes 184328 | tf_op jit(solution)/shard_map/ppermute | solution.py:19
  182.6 49.3 %collective-permute-start.6 = (f32[4,10,1,3,128]{4,0,2,1,3:T(4,128)S(1)}, f32[4,10,1,3,128]{4,0,2,1,3:T(4,128)S(1)}, u32[]{:S(2)}, u32[]{:S(2)}) collective-permute-start(f32[4,10,1,3,128]{4,0,2,1,3:T(4,128)S(1)} %get-tuple-element.21), channel_id=1, source_target_pairs={{0,1},{1,2},{2,3},{3,4},{4,5},{5,6},{6,7},{8,9},{9,10},{10,11},{11... | collective-permute-start | bytes 184328 | tf_op jit(solution)/shard_map/ppermute | solution.py:17
  232.6 4.2 %copy-start.5 = (f32[256,384]{1,0:T(8,128)S(1)}, f32[256,384]{1,0:T(8,128)}, u32[]{:S(2)}) copy-start(f32[256,384]{1,0:T(8,128)} %copy-done.4) | copy-start | bytes 1179652
  232.7 4.2 %slice-start = ((f32[4,10,1,3,128]{4,0,2,1,3:T(4,128)}), f32[4,8,1,3,128]{4,0,2,1,3:T(4,128)S(1)}, s32[]{:S(2)}) async-start(f32[4,10,1,3,128]{4,0,2,1,3:T(4,128)} %copy-done.14), calls=%async_computation.1 | async-start | bytes 98304 | tf_op jit(solution)/shard_map/slice | solution.py:62
  232.7 4.2 %slice-start.1 = ((f32[4,10,1,3,128]{4,0,2,1,3:T(4,128)}), f32[4,8,1,3,128]{4,0,2,1,3:T(4,128)S(1)}, s32[]{:S(2)}) async-start(f32[4,10,1,3,128]{4,0,2,1,3:T(4,128)} %copy-done.15), calls=%async_computation.2 | async-start | bytes 98304 | tf_op jit(solution)/shard_map/slice | solution.py:62
  233.6 3.3 copy-start.3
  236.9 123.1 %copy-start.9 = (f32[4,8,8,3,128]{4,2,3,1,0:T(8,128)S(1)}, f32[4,8,8,3,128]{4,2,3,1,0:T(8,128)}, u32[]{:S(2)}) copy-start(f32[4,8,8,3,128]{4,2,3,1,0:T(8,128)} %param.13) | copy-start | bytes 1179652
  (7 other events, 7.2 us)
